TPU v7x, 32 devices: a whole 2x2x4 slice. The times are simulated.
32 devices in a mesh: row: 4 (over y, x), col: 8 (over z, core).
Axes of the slice: x: 2, y: 2, z: 4, core: 2. Of those that a mesh axis runs over, the one named last changes fastest.
Arguments:
- activations: bfloat16 [256, 16384], P(None, 'row'), may hold values from -3 to 3
- cotangent: bfloat16 [256, 16384], P(None, 'row'), may hold values from -0.59765625 to 0.59765625
- forget: int32 [256], replicated, may hold values 0 or 1
- lengths: int32 [4, 4], P('row'), may hold values from 1 to 32, 64 in all within a row
- query_weight: bfloat16 [16384, 8192], P('row', 'col'), may hold values from -0.046875 to 0.046875
- key_weight: bfloat16 [16384, 512], P('row'), may hold values from -0.046875 to 0.046875
- value_weight: bfloat16 [16384, 512], P('row'), may hold values from -0.046875 to 0.046875
- output_projection_weight: bfloat16 [8192, 16384], P('col', 'row'), may hold values from -0.0625 to 0.0625
- query_down: bfloat16 [16384, 32], P('row'), may hold values from -0.046875 to 0.046875
- query_up: bfloat16 [32, 8192], P(None, 'col'), may hold values from -1 to 1
- output_down: bfloat16 [8192, 32], P('col'), may hold values from -0.0625 to 0.0625
- output_up: bfloat16 [32, 16384], P(None, 'row'), may hold values from -1 to 1
Outputs:
- query_down_gradient: float32 [16384, 32], P('row')
- query_up_gradient: float32 [32, 8192], P(None, 'col')
- output_down_gradient: float32 [8192, 32], P('col')
- output_up_gradient: float32 [32, 16384], P(None, 'row')
Inputs may be any that keep to these rules, and one draw needn't show every extreme that they name: In every row of lengths the 4 values sum to 64, and the largest is exactly 32.
All inputs are finite; a program needn't handle non-finite values.
Results may differ from a plain program's by a relative error of at most 0.025.
Values may be sent and summed in bfloat16 or wider, within the bound.
A program may use at most 128 MiB of HBM per device.

v0:
```python
import math
import jax
import jax.numpy as jnp
from jax import lax
from jax.sharding import PartitionSpec as P

HD = 128
HEADS = 64
KVH = 4
adapter_scale = 0.5
highest_precision = lax.Precision.HIGHEST


def row_contraction(left, right):
    return lax.dot_general(
        left, right, (((1,), (1,)), ((), ())), preferred_element_type=jnp.float32
    )


def token_contraction(left, right):
    return lax.dot_general(
        left, right, (((0,), (0,)), ((), ())), preferred_element_type=jnp.float32
    )


def local(
    activations,
    cotangent,
    forget,
    lengths,
    query_weight,
    key_weight,
    value_weight,
    output_projection_weight,
    query_down,
    query_up,
    output_down,
    output_up,
):
    row_index = lax.axis_index("row")
    col_index = lax.axis_index("col")
    tok_blk = activations.shape[0] // lax.axis_size("row")
    query_cols = query_weight.shape[1]
    heads_dev = query_cols // HD
    group_index = col_index * heads_dev // (HEADS // KVH)
    inverse = 1.0 / math.sqrt(HD)
    up_projection_broad = query_up.astype(jnp.float32)
    down_projection_broad = output_down.astype(jnp.float32)
    key_slice = lax.dynamic_slice_in_dim(key_weight, group_index * HD, HD, 1)
    value_slice = lax.dynamic_slice_in_dim(value_weight, group_index * HD, HD, 1)
    kv_cols = key_slice.shape[1]
    block_of_rows = activations
    reduced_result = jnp.dot(block_of_rows, query_down, preferred_element_type=jnp.float32)
    query_partial_term = jnp.dot(block_of_rows, query_weight, preferred_element_type=jnp.float32)
    query_partial_term = query_partial_term + adapter_scale * jnp.dot(
        reduced_result, up_projection_broad, precision=highest_precision
    )
    key_term = jnp.dot(block_of_rows, key_slice, preferred_element_type=jnp.float32)
    value_term = jnp.dot(block_of_rows, value_slice, preferred_element_type=jnp.float32)
    summed = lax.psum_scatter(
        jnp.concatenate([query_partial_term, key_term, value_term, reduced_result], axis=1).astype(
            jnp.bfloat16
        ),
        "row",
        scatter_dimension=0,
        tiled=True,
    ).astype(jnp.float32)
    query_heads = summed[:, :query_cols].astype(jnp.bfloat16).reshape(tok_blk, heads_dev, HD)
    key_part = summed[:, query_cols : query_cols + kv_cols].astype(jnp.bfloat16)
    value_part = summed[:, query_cols + kv_cols : query_cols + 2 * kv_cols].astype(jnp.bfloat16)
    input_lowrank_factor = summed[:, query_cols + 2 * kv_cols :]
    seg_ends = jnp.cumsum(lengths[0])
    position = jnp.arange(tok_blk, dtype=jnp.int32)
    segment = jnp.sum((position[:, None] >= seg_ends[None, :]).astype(jnp.int32), axis=1)
    allowed = (segment[:, None] == segment[None, :]) & (position[None, :] <= position[:, None])
    scores = (
        jnp.einsum("qhd,kd->hqk", query_heads, key_part, preferred_element_type=jnp.float32)
        * inverse
    )
    numerator = jnp.where(allowed[None], jnp.exp(scores), 0.0)
    softmax = numerator / jnp.sum(numerator, axis=2, keepdims=True)
    weights = softmax.astype(jnp.bfloat16)
    hidden_state = jnp.einsum(
        "hqk,kd->qhd", weights, value_part, preferred_element_type=jnp.float32
    )
    hidden_state = hidden_state.reshape(tok_blk, query_cols).astype(jnp.bfloat16)
    sign_flip = (1 - 2 * forget).astype(jnp.bfloat16)
    output_gradient = cotangent * sign_flip[:, None]
    block_of_rows = output_gradient
    reduced_result = row_contraction(block_of_rows, output_up)
    hidden_state_term = row_contraction(
        block_of_rows, output_projection_weight
    ) + adapter_scale * jnp.dot(
        reduced_result, down_projection_broad.T, precision=highest_precision
    )
    backward = lax.psum_scatter(
        jnp.concatenate([hidden_state_term, reduced_result], axis=1).astype(jnp.bfloat16),
        "row",
        scatter_dimension=0,
        tiled=True,
    ).astype(jnp.float32)
    hidden_grad = backward[:, :query_cols].astype(jnp.bfloat16).reshape(tok_blk, heads_dev, HD)
    gradient_lowrank_factor = backward[:, query_cols:]
    prob_grad = jnp.einsum(
        "qhd,kd->hqk", hidden_grad, value_part, preferred_element_type=jnp.float32
    )
    score_grad = softmax * (prob_grad - jnp.sum(prob_grad * softmax, axis=2, keepdims=True))
    query_gradient = (
        jnp.einsum(
            "hqk,kd->qhd", score_grad, key_part.astype(jnp.float32), precision=highest_precision
        )
        * inverse
    )
    query_gradient = query_gradient.reshape(tok_blk, query_cols)
    query_lowrank_factor = jnp.dot(
        query_gradient, up_projection_broad.T, precision=highest_precision
    )
    hidden_state_factor = jnp.dot(hidden_state, output_down, preferred_element_type=jnp.float32)
    up_projection_piece = adapter_scale * jnp.dot(
        input_lowrank_factor.T, query_gradient, precision=highest_precision
    )
    down_projection_piece = adapter_scale * jnp.dot(
        hidden_state.astype(jnp.float32).T, gradient_lowrank_factor, precision=highest_precision
    )
    query_up_gradient, output_down_gradient = (
        lax.psum(up_projection_piece.astype(jnp.bfloat16), "row").astype(jnp.float32),
        lax.psum(down_projection_piece.astype(jnp.bfloat16), "row").astype(jnp.float32),
    )
    zero_rows = jnp.zeros((activations.shape[0], query_lowrank_factor.shape[1]), jnp.float32)
    first_token = row_index * tok_blk
    query_padded = lax.dynamic_update_slice_in_dim(zero_rows, query_lowrank_factor, first_token, 0)
    hidden_padded = lax.dynamic_update_slice_in_dim(zero_rows, hidden_state_factor, first_token, 0)
    query_total, hidden_total = lax.psum((query_padded, hidden_padded), ("row", "col"))
    query_everywhere = query_total.astype(jnp.bfloat16)
    hidden_state_everywhere = hidden_total.astype(jnp.bfloat16)
    query_down_gradient = adapter_scale * token_contraction(activations, query_everywhere)
    output_up_gradient = adapter_scale * token_contraction(hidden_state_everywhere, output_gradient)
    return (query_down_gradient, query_up_gradient, output_down_gradient, output_up_gradient)


def solution(mesh):
    placed = (
        P(None, "row"),
        P(None, "row"),
        P(),
        P("row", None),
        P("row", "col"),
        P("row", None),
        P("row", None),
        P("col", "row"),
        P("row", None),
        P(None, "col"),
        P("col", None),
        P(None, "row"),
    )
    return jax.shard_map(
        local,
        mesh=mesh,
        in_specs=placed,
        out_specs=(P("row", None), P(None, "col"), P("col", None), P(None, "row")),
        check_vma=False,
    )
```

profile of v0, /device:TPU:0, one launch (start us, length us, event | category | flops | bytes accessed | tf_op | source)
XLA Modules:
  0.0 180.6 jit_solution(12886477900674417634)
XLA Ops:
  7.2 1.5 copy-done
  8.8 1.7 fusion.58
  10.6 1.9 %fusion.17 = bf16[256,128]{1,0:T(8,128)(2,1)S(1)} fusion(bf16[256,4096]{1,0:T(8,128)(2,1)S(1)} %copy-done, bf16[4096,512]{1,0:T(8,128)(2,1)} %param.17, s32[]{:T(128)S(6)} %select_n.18), kind=kOutput, calls=%fused_computation.29 | convolution fusion | flops 268468224 | bytes 3211268 | tf_op jit(solution)/shard_map/dot_general | solution.py:58
  12.5 1.9 %fusion.18 = bf16[256,128]{1,0:T(8,128)(2,1)S(1)} fusion(bf16[256,4096]{1,0:T(8,128)(2,1)S(1)} %copy-done, bf16[4096,512]{1,0:T(8,128)(2,1)} %param.18, s32[]{:T(128)S(6)} %select_n.18), kind=kOutput, calls=%fused_computation.30 | convolution fusion | flops 268468224 | bytes 3211268 | tf_op jit(solution)/shard_map/dot_general | solution.py:59
  14.4 5.7 %fusion.60 = f32[256,1024]{1,0:T(8,128)S(1)} fusion(bf16[256,4096]{1,0:T(8,128)(2,1)S(1)} %copy-done, bf16[4096,1024]{1,0:T(8,128)(2,1)} %param.16), kind=kOutput, calls=%fused_computation.79 | convolution fusion | flops 2147483648 | bytes 11534336 | tf_op jit(solution)/shard_map/dot_general | solution.py:54
  20.2 0.7 fusion.8
  20.9 0.9 pad_maximum_fusion
  21.9 2.4 %fusion.59 = (bf16[256,32]{0,1:T(8,128)(2,1)S(1)}, f32[256,32]{0,1:T(8,128)S(1)}) fusion(bf16[32,4096]{1,0:T(8,128)(2,1)S(1)} %copy-done.3, bf16[256,4096]{1,0:T(8,128)(2,1)} %param.13, bf16[256]{0:T(256)(128)(2,1)S(1)} %subtract_convert_fusion), kind=kOutput, calls=%fused_computation.78 | convolution fusion | flops 68165632 | bytes 2408960 | tf_op jit(solution)/shard_map/dot_general | solution.py:15
  24.5 6.4 %fusion.4 = f32[256,1024]{1,0:T(8,128)S(1)} fusion(bf16[1024,4096]{1,0:T(8,128)(2,1)} %param.19, bf16[256,4096]{1,0:T(8,128)(2,1)} %param.13, bf16[256]{0:T(256)(128)(2,1)S(1)} %subtract_convert_fusion), kind=kOutput, calls=%fused_computation.6 | convolution fusion | flops 2148532224 | bytes 11534848 | tf_op jit(solution)/shard_map/dot_general | solution.py:15
  31.5 0.9 pad_maximum_fusion.1
  32.8 17.6 %reduce-scatter.3.cloned.1.call-done = bf16[64,1312]{1,0:T(8,128)(2,1)} async-done(((bf16[256,1312]{1,0:T(8,128)(2,1)}), bf16[64,1312]{1,0:T(8,128)(2,1)}) %reduce-scatter.3.cloned.1.call-update) | async-done | bytes 167952 | tf_op jit(solution)/shard_map/reduce_scatter | solution.py:60
  50.4 1.2 fusion.41
  51.7 0.9 fusion.14
  52.7 25.9 %reduce-scatter.5.cloned.1.call-done = bf16[64,1056]{1,0:T(8,128)(2,1)} async-done(((bf16[256,1056]{1,0:T(8,128)(2,1)}), bf16[64,1056]{1,0:T(8,128)(2,1)}) %reduce-scatter.5.cloned.1.call-update) | async-done | bytes 135184 | tf_op jit(solution)/shard_map/reduce_scatter | solution.py:96
  78.7 1.2 multiply_reduce_fusion
  79.8 1.1 fusion.10
  82.0 39.9 %all-reduce = (bf16[256,32]{0,1:T(8,128)(2,1)S(1)}, bf16[256,32]{0,1:T(8,128)(2,1)S(1)}) all-reduce(f32[256,32]{0,1:T(8,128)S(1)} %dynamic_update_slice.6, f32[256,32]{0,1:T(8,128)S(1)} %dynamic_update_slice.7), channel_id=1, replica_groups=mesh['row'=4,'col'=8] {'row','col'}, use_global_device_ids=true, to_apply=%region_6.7 | all-reduce | flops 16384 | bytes 98304 | tf_op jit(solution)/shard_map/psum | solution.py:133
  121.9 2.9 %convolution_multiply_fusion = f32[32,4096]{1,0:T(8,128)} fusion(bf16[256,4096]{1,0:T(8,128)(2,1)} %param.13, bf16[256]{0:T(256)(128)(2,1)S(1)} %subtract_convert_fusion, bf16[256,32]{0,1:T(8,128)(2,1)S(1)} %get-tuple-element.5), kind=kOutput, calls=%fused_computation | convolution fusion | flops 68288512 | bytes 2638336 | tf_op jit(solution)/shard_map/dot_general | solution.py:21
  124.8 1.6 fusion.16
  126.4 1.6 fusion.15
  128.0 1.3 fusion
  129.2 41.8 %all-reduce.4.cloned.1.call-done = (bf16[32,1024]{1,0:T(8,128)(2,1)}, bf16[1024,32]{0,1:T(8,128)(2,1)}) async-done(((bf16[32,1024]{1,0:T(8,128)(2,1)}, bf16[1024,32]{0,1:T(8,128)(2,1)}), (bf16[32,1024]{1,0:T(8,128)(2,1)}, bf16[1024,32]{0,1:T(8,128)(2,1)})) %all-reduce.4.cloned.1.call-update) | async-done | bytes 131088 | tf_op jit(solution)/shard_map/psum | solution.py:126
  171.0 1.5 convert_element_type.52
  172.5 1.5 convert_element_type.58
  (30 shorter events, 2.5 us)
Async XLA Ops:
  7.2 1.6 copy-start
  7.2 43.3 %reduce-scatter.3.cloned.1.call-start = ((), (), s32[]{:S(2)}) async-start(), calls=%async_computation.2 | async-start | bytes 901120 | tf_op jit(solution)/shard_map/reduce_scatter | solution.py:60
  14.4 5.8 %copy-start.1 = (bf16[32,1024]{1,0:T(8,128)(2,1)S(1)}, bf16[32,1024]{1,0:T(8,128)(2,1)}, u32[]{:S(2)}) copy-start(bf16[32,1024]{1,0:T(8,128)(2,1)} %param.21) | copy-start | bytes 196612
  20.2 1.7 copy-start.4
  20.2 1.7 copy-start.3
  21.8 56.8 %reduce-scatter.5.cloned.1.call-start = ((), (), s32[]{:S(2)}) async-start(), calls=%async_computation.3 | async-start | bytes 737280 | tf_op jit(solution)/shard_map/reduce_scatter | solution.py:96
  24.5 6.4 %copy-start.2 = (bf16[1024,32]{0,1:T(8,128)(2,1)S(1)}, bf16[1024,32]{0,1:T(8,128)(2,1)}, u32[]{:S(2)}) copy-start(bf16[1024,32]{0,1:T(8,128)(2,1)} %param.22) | copy-start | bytes 196612
  30.9 1.6 copy-start.5
  32.4 138.6 %all-reduce.4.cloned.1.call-start = ((), (), s32[]{:S(2)}) async-start(), calls=%async_computation.4 | async-start | bytes 262144 | tf_op jit(solution)/shard_map/psum | solution.py:126
Sparse Core Ops, SparseCore 0:
  22.0 28.4 reduce-scatter.2
  53.6 25.0 reduce-scatter.4
  128.1 42.8 all-reduce.3
where the time goes:
time: 181 us
  waiting for transfers between devices  85.3 us (47%)
  blocking collectives  39.9 us (22%)
  matrix products  33.5 us (19%)
  between operations  14 us (8%)
  other arithmetic  5.14 us (3%)
  local copies, waits for them, and re-layouts  2.51 us (1%)
    psum x1, waiting for transfers between devices, local(): lax.psum(up_projection_piece.astype(jnp.bfloat16), 'row')  41.8 us
    psum x1, blocking collectives, local(): lax.psum((query_padded, hidden_padded), ('row', 'col'))  39.9 us
    reduce_scatter x1, waiting for transfers between devices, local(): lax.psum_scatter(jnp.concatenate([hidden_state_term, reduced_result], axi...  25.9 us
    reduce_scatter x1, waiting for transfers between devices, local(): lax.psum_scatter(jnp.concatenate([query_partial_term, key_term, value_ter...  17.6 us
    dot_general x2, matrix products, row_contraction(): lax.dot_general(left, right, (((1,), (1,)), ((), ())), preferred_element_...  8.79 us
    dot_general x1, matrix products, local(): jnp.dot(block_of_rows, query_weight, preferred_element_type=jnp.float32)  5.74 us
    dot_general x2, matrix products, token_contraction(): lax.dot_general(left, right, (((0,), (0,)), ((), ())), preferred_element_...  4.2 us
  transfers between devices with their start and end apart: 3, of which 3 were waited for; matrix products, arithmetic and copies ran while one was open for 8% of the time, Pallas kernels for 0%

commit v1 on v0

--- a/solution.py
+++ b/solution.py
@@ -130,7 +130,7 @@
     first_token = row_index * tok_blk
     query_padded = lax.dynamic_update_slice_in_dim(zero_rows, query_lowrank_factor, first_token, 0)
     hidden_padded = lax.dynamic_update_slice_in_dim(zero_rows, hidden_state_factor, first_token, 0)
-    query_total, hidden_total = lax.psum((query_padded, hidden_padded), ("row", "col"))
+    query_total, hidden_total = lax.psum(lax.psum((query_padded, hidden_padded), "col"), "row")
     query_everywhere = query_total.astype(jnp.bfloat16)
     hidden_state_everywhere = hidden_total.astype(jnp.bfloat16)
     query_down_gradient = adapter_scale * token_contraction(activations, query_everywhere)

time: 181 us -> 192 us (1.061)
  waiting for transfers between devices: 85.3 us -> 118 us
  blocking collectives: 39.9 us -> 17.5 us
    psum x0 -> x1, waiting for transfers between devices: none -> 50.9 us  [local(): lax.psum((query_padded, hidden_padded), 'col')]
    psum x1, blocking collectives: 39.9 us -> 17.5 us  [local(): lax.psum(lax.psum((query_padded, hidden_padded), 'col'), 'row')]
    psum x1, waiting for transfers between devices: 41.8 us -> 23.1 us  [local(): lax.psum(up_projection_piece.astype(jnp.bfloat16), 'row')]
  transfers between devices with their start and end apart: 3 -> 4, of which waited for: 3 -> 4; matrix products, arithmetic and copies ran while one was open for 8% -> 11% of each run, Pallas kernels for 0% -> 0%
where the time goes in v1:
time: 192 us; the launch traced here: 191 us
  waiting for transfers between devices  118 us (61%)
  matrix products  33.5 us (17%)
  blocking collectives  17.5 us (9%)
  between operations  14 us (7%)
  other arithmetic  5.16 us (3%)
  local copies, waits for them, and re-layouts  3.13 us (2%)
    psum x1, waiting for transfers between devices, local(): lax.psum((query_padded, hidden_padded), 'col')  50.9 us
    reduce_scatter x1, waiting for transfers between devices, local(): lax.psum_scatter(jnp.concatenate([hidden_state_term, reduced_result], axi...  25.9 us
    psum x1, waiting for transfers between devices, local(): lax.psum(up_projection_piece.astype(jnp.bfloat16), 'row')  23.1 us
    reduce_scatter x1, waiting for transfers between devices, local(): lax.psum_scatter(jnp.concatenate([query_partial_term, key_term, value_ter...  17.6 us
    psum x1, blocking collectives, local(): lax.psum(lax.psum((query_padded, hidden_padded), 'col'), 'row')  17.5 us
    dot_general x2, matrix products, row_contraction(): lax.dot_general(left, right, (((1,), (1,)), ((), ())), preferred_element_...  8.78 us
    dot_general x1, matrix products, local(): jnp.dot(block_of_rows, query_weight, preferred_element_type=jnp.float32)  5.74 us
    dot_general x2, matrix products, token_contraction(): lax.dot_general(left, right, (((0,), (0,)), ((), ())), preferred_element_...  4.2 us
  transfers between devices with their start and end apart: 4, of which 4 were waited for; matrix products, arithmetic and copies ran while one was open for 11% of the time, Pallas kernels for 0%

profile of v1, /device:TPU:0, one launch (start us, length us, event | category | flops | bytes accessed | tf_op | source)
XLA Modules:
  0.0 191.1 jit_solution(12919430982076208088)
XLA Ops:
  7.2 1.5 copy-done
  8.8 1.7 fusion.58
  10.6 1.9 %fusion.17 = bf16[256,128]{1,0:T(8,128)(2,1)S(1)} fusion(bf16[256,4096]{1,0:T(8,128)(2,1)S(1)} %copy-done, bf16[4096,512]{1,0:T(8,128)(2,1)} %param.17, s32[]{:T(128)S(6)} %select_n.18), kind=kOutput, calls=%fused_computation.29 | convolution fusion | flops 268468224 | bytes 3211268 | tf_op jit(solution)/shard_map/dot_general | solution.py:58
  12.5 1.9 %fusion.18 = bf16[256,128]{1,0:T(8,128)(2,1)S(1)} fusion(bf16[256,4096]{1,0:T(8,128)(2,1)S(1)} %copy-done, bf16[4096,512]{1,0:T(8,128)(2,1)} %param.18, s32[]{:T(128)S(6)} %select_n.18), kind=kOutput, calls=%fused_computation.30 | convolution fusion | flops 268468224 | bytes 3211268 | tf_op jit(solution)/shard_map/dot_general | solution.py:59
  14.4 5.7 %fusion.60 = f32[256,1024]{1,0:T(8,128)S(1)} fusion(bf16[256,4096]{1,0:T(8,128)(2,1)S(1)} %copy-done, bf16[4096,1024]{1,0:T(8,128)(2,1)} %param.16), kind=kOutput, calls=%fused_computation.79 | convolution fusion | flops 2147483648 | bytes 11534336 | tf_op jit(solution)/shard_map/dot_general | solution.py:54
  20.9 0.9 pad_maximum_fusion
  21.9 2.4 %fusion.59 = (bf16[256,32]{0,1:T(8,128)(2,1)S(1)}, f32[256,32]{0,1:T(8,128)S(1)}) fusion(bf16[32,4096]{1,0:T(8,128)(2,1)S(1)} %copy-done.5, bf16[256,4096]{1,0:T(8,128)(2,1)} %param.13, bf16[256]{0:T(256)(128)(2,1)S(1)} %subtract_convert_fusion), kind=kOutput, calls=%fused_computation.78 | convolution fusion | flops 68165632 | bytes 2408960 | tf_op jit(solution)/shard_map/dot_general | solution.py:15
  24.5 6.4 %fusion.4 = f32[256,1024]{1,0:T(8,128)S(1)} fusion(bf16[1024,4096]{1,0:T(8,128)(2,1)} %param.19, bf16[256,4096]{1,0:T(8,128)(2,1)} %param.13, bf16[256]{0:T(256)(128)(2,1)S(1)} %subtract_convert_fusion), kind=kOutput, calls=%fused_computation.6 | convolution fusion | flops 2148532224 | bytes 11534848 | tf_op jit(solution)/shard_map/dot_general | solution.py:15
  31.5 0.9 pad_maximum_fusion.1
  32.9 17.6 %reduce-scatter.3.cloned.1.call-done = bf16[64,1312]{1,0:T(8,128)(2,1)} async-done(((bf16[256,1312]{1,0:T(8,128)(2,1)}), bf16[64,1312]{1,0:T(8,128)(2,1)}) %reduce-scatter.3.cloned.1.call-update) | async-done | bytes 167952 | tf_op jit(solution)/shard_map/reduce_scatter | solution.py:60
  50.5 1.2 fusion.41
  51.7 0.9 fusion.14
  52.7 25.9 %reduce-scatter.5.cloned.1.call-done = bf16[64,1056]{1,0:T(8,128)(2,1)} async-done(((bf16[256,1056]{1,0:T(8,128)(2,1)}), bf16[64,1056]{1,0:T(8,128)(2,1)}) %reduce-scatter.5.cloned.1.call-update) | async-done | bytes 135184 | tf_op jit(solution)/shard_map/reduce_scatter | solution.py:96
  78.7 1.2 multiply_reduce_fusion
  79.8 1.1 fusion.10
  82.7 1.6 fusion.15
  84.3 1.6 fusion.16
  85.9 50.9 %all-reduce.6.cloned.1.call-done = (f32[256,32]{0,1:T(8,128)}, f32[256,32]{0,1:T(8,128)}) async-done(((f32[256,32]{0,1:T(8,128)}, f32[256,32]{0,1:T(8,128)}), (f32[256,32]{0,1:T(8,128)}, f32[256,32]{0,1:T(8,128)})) %all-reduce.6.cloned.1.call-update) | async-done | bytes 65552 | tf_op jit(solution)/shard_map/psum | solution.py:133
  136.7 17.5 %all-reduce.1 = (bf16[256,32]{0,1:T(8,128)(2,1)S(1)}, bf16[256,32]{0,1:T(8,128)(2,1)S(1)}) all-reduce(f32[256,32]{0,1:T(8,128)} %get-tuple-element.4, f32[256,32]{0,1:T(8,128)} %get-tuple-element.5), channel_id=1, replica_groups=mesh['row'=4,'col'=8] {'row'}, use_global_device_ids=true, to_apply=%region_7.8 | all-reduce | flops 16384 | bytes 98304 | tf_op jit(solution)/shard_map/psum | solution.py:133
  154.2 2.9 %convolution_multiply_fusion = f32[32,4096]{1,0:T(8,128)} fusion(bf16[256,4096]{1,0:T(8,128)(2,1)} %param.13, bf16[256]{0:T(256)(128)(2,1)S(1)} %subtract_convert_fusion, bf16[256,32]{0,1:T(8,128)(2,1)S(1)} %get-tuple-element.7), kind=kOutput, calls=%fused_computation | convolution fusion | flops 68288512 | bytes 2638336 | tf_op jit(solution)/shard_map/dot_general | solution.py:21
  157.2 1.3 fusion
  158.4 23.1 %all-reduce.8.cloned.1.call-done = (bf16[32,1024]{1,0:T(8,128)(2,1)}, bf16[1024,32]{0,1:T(8,128)(2,1)}) async-done(((bf16[32,1024]{1,0:T(8,128)(2,1)}, bf16[1024,32]{0,1:T(8,128)(2,1)}), (bf16[32,1024]{1,0:T(8,128)(2,1)}, bf16[1024,32]{0,1:T(8,128)(2,1)})) %all-reduce.8.cloned.1.call-update) | async-done | bytes 131088 | tf_op jit(solution)/shard_map/psum | solution.py:126
  181.5 1.5 convert_element_type.52
  183.0 1.5 convert_element_type.58
  (37 shorter events, 3.9 us)
Async XLA Ops:
  7.2 1.6 copy-start
  7.2 43.3 %reduce-scatter.3.cloned.1.call-start = ((), (), s32[]{:S(2)}) async-start(), calls=%async_computation.2 | async-start | bytes 901120 | tf_op jit(solution)/shard_map/reduce_scatter | solution.py:60
  14.4 5.8 %copy-start.1 = (bf16[32,1024]{1,0:T(8,128)(2,1)S(1)}, bf16[32,1024]{1,0:T(8,128)(2,1)}, u32[]{:S(2)}) copy-start(bf16[32,1024]{1,0:T(8,128)(2,1)} %param.21) | copy-start | bytes 196612
  20.2 1.7 copy-start.6
  20.2 1.7 copy-start.5
  21.8 56.8 %reduce-scatter.5.cloned.1.call-start = ((), (), s32[]{:S(2)}) async-start(), calls=%async_computation.3 | async-start | bytes 737280 | tf_op jit(solution)/shard_map/reduce_scatter | solution.py:96
  24.5 6.4 %copy-start.4 = (bf16[1024,32]{0,1:T(8,128)(2,1)S(1)}, bf16[1024,32]{0,1:T(8,128)(2,1)}, u32[]{:S(2)}) copy-start(bf16[1024,32]{0,1:T(8,128)(2,1)} %param.22) | copy-start | bytes 196612
  30.9 1.6 copy-start.7
  32.4 104.3 %all-reduce.6.cloned.1.call-start = ((), (), s32[]{:S(2)}) async-start(), calls=%async_computation.4 | async-start | bytes 131072 | tf_op jit(solution)/shard_map/psum | solution.py:133
  81.6 0.6 copy-start.3
  82.0 0.6 copy-start.2
  82.6 98.9 %all-reduce.8.cloned.1.call-start = ((), (), s32[]{:S(2)}) async-start(), calls=%async_computation.5 | async-start | bytes 262144 | tf_op jit(solution)/shard_map/psum | solution.py:126
Sparse Core Ops, SparseCore 0:
  22.0 28.4 reduce-scatter.2
  53.6 25.0 reduce-scatter.4
  82.7 53.9 all-reduce.5
  140.3 41.2 all-reduce.7
